TPU v7x, 256 devices: a whole 4x4x8 slice. The times are simulated.
256 devices in a mesh: row: 8 (over x, core), col: 32 (over z, y).
Axes of the slice: x: 4, y: 4, z: 8, core: 2. Of those that a mesh axis runs over, the one named last changes fastest.
Arguments:
- inputs: bfloat16 [1024, 8192], P('col', 'row'), may hold values from -6 to 6
- target: bfloat16 [1024, 8192], P(None, 'row'), may hold values from -6 to 6
- gate_weight: bfloat16 [8192, 16384], P('row', 'col'), may hold values from -0.0625 to 0.0625
- up_weight: bfloat16 [8192, 16384], P('row', 'col'), may hold values from -0.0625 to 0.0625
- down_weight: bfloat16 [16384, 8192], P('col', 'row'), may hold values from -0.046875 to 0.046875
Outputs:
- output: bfloat16 [1024, 8192], P('col', 'row')
- grad_inputs: bfloat16 [1024, 8192], P('col', 'row')
- grad_gate_weight: bfloat16 [8192, 16384], P('row', 'col')
- grad_up_weight: bfloat16 [8192, 16384], P('row', 'col')
- grad_down_weight: bfloat16 [16384, 8192], P('col', 'row')
All inputs are finite; a program needn't handle non-finite values.
Results may differ from a plain program's by a relative error of at most 0.0065.
Values may be sent and summed in bfloat16 or wider, within the bound.
No kernel may reach another device: no remote copies, remote signals or barrier semaphores. Data moves between devices by JAX's collectives and lax.ppermute only.
A program may use at most 64 MiB of HBM per device.

v0:
```python
import jax
import jax.numpy as jnp
from jax import lax
from jax.sharding import PartitionSpec as P


def contract_first(left, right):
    return lax.dot_general(
        left, right, (((0,), (0,)), ((), ())), preferred_element_type=jnp.float32
    )


def contract_last(left, right):
    return lax.dot_general(
        left, right, (((1,), (1,)), ((), ())), preferred_element_type=jnp.float32
    )


def gate_grads(hidden_grad, gate_act, up_act):
    sigma = jax.nn.sigmoid(gate_act)
    silu_val = gate_act * sigma
    grad_gate = (hidden_grad * up_act * sigma * (1.0 + gate_act * (1.0 - sigma))).astype(
        jnp.bfloat16
    )
    grad_up = (hidden_grad * silu_val).astype(jnp.bfloat16)
    return (grad_gate, grad_up)


def body(inputs, target, gate_weight, up_weight, down_weight):
    tokens_all = lax.all_gather(inputs, "col", axis=0, tiled=True)
    gate_part = jnp.dot(tokens_all, gate_weight, preferred_element_type=jnp.float32)
    up_part = jnp.dot(tokens_all, up_weight, preferred_element_type=jnp.float32)
    gate_own, up_own = (
        lax.psum_scatter(gate_part, "row", scatter_dimension=0, tiled=True),
        lax.psum_scatter(up_part, "row", scatter_dimension=0, tiled=True),
    )
    hidden_own = (jax.nn.silu(gate_own) * up_own).astype(jnp.bfloat16)
    hidden_all = lax.all_gather(hidden_own, "row", axis=0, tiled=True)
    result_part = jnp.dot(hidden_all, down_weight, preferred_element_type=jnp.float32)
    tok_col = inputs.shape[0]
    offset = lax.axis_index("col") * tok_col
    result_own = lax.psum_scatter(result_part, "col", scatter_dimension=0, tiled=True)
    target_own = lax.dynamic_slice_in_dim(target, offset, tok_col, 0)
    error_own = (result_own - target_own.astype(jnp.float32)).astype(jnp.bfloat16)
    output = result_own.astype(jnp.bfloat16)
    error_all = lax.all_gather(error_own, "col", axis=0, tiled=True)
    grad_down_weight = contract_first(hidden_all, error_all).astype(jnp.bfloat16)
    hidden_grad_part = contract_last(error_all, down_weight)
    hidden_grad = lax.psum_scatter(hidden_grad_part, "row", scatter_dimension=0, tiled=True)
    gate_grad_own, up_grad_own = gate_grads(hidden_grad, gate_own, up_own)
    gate_grad_all, up_grad_all = (
        lax.all_gather(gate_grad_own, "row", axis=0, tiled=True),
        lax.all_gather(up_grad_own, "row", axis=0, tiled=True),
    )
    grad_gate_weight = contract_first(tokens_all, gate_grad_all).astype(jnp.bfloat16)
    grad_up_weight = contract_first(tokens_all, up_grad_all).astype(jnp.bfloat16)
    input_grad_part = contract_last(gate_grad_all, gate_weight) + contract_last(
        up_grad_all, up_weight
    )
    grad_inputs = lax.psum_scatter(input_grad_part, "col", scatter_dimension=0, tiled=True).astype(
        jnp.bfloat16
    )
    return (output, grad_inputs, grad_gate_weight, grad_up_weight, grad_down_weight)


def solution(mesh):
    placed = (P("col", "row"), P(None, "row"), P("row", "col"), P("row", "col"), P("col", "row"))
    return jax.shard_map(
        body,
        mesh=mesh,
        in_specs=placed,
        out_specs=(
            P("col", "row"),
            P("col", "row"),
            P("row", "col"),
            P("row", "col"),
            P("col", "row"),
        ),
        check_vma=False,
    )
```

profile of v0, /device:TPU:4, one launch (start us, length us, event | category | flops | bytes accessed | tf_op | source)
XLA Modules:
  0.0 833.2 jit_solution(12145454576737987996)
XLA Ops:
  7.2 0.0 copy-start
  7.2 0.0 all-gather.6.cloned.1.call-start
  7.2 0.7 all-gather.6.cloned.1.call-update
  7.9 0.0 reduce-scatter.8.cloned.1.call-start
  8.0 83.7 %all-gather.6.cloned.1.call-done = bf16[1024,1024]{1,0:T(8,128)(2,1)} async-done(((bf16[32,1024]{1,0:T(8,128)(2,1)}), bf16[1024,1024]{1,0:T(8,128)(2,1)}) %all-gather.6.cloned.1.call-update) | async-done | bytes 2097168 | tf_op jit(solution)/shard_map/all_gather | solution.py:30
  91.7 4.4 fusion.4
  96.1 0.0 reduce-scatter.8.cloned.1.call-update
  96.1 0.0 reduce-scatter.6.cloned.1.call-start
  96.2 1.5 copy-done.1
  97.7 3.8 fusion.3
  101.5 0.0 reduce-scatter.6.cloned.1.call-update
  101.5 0.0 all-gather.8.cloned.1.call-start
  101.5 23.3 %reduce-scatter.8.cloned.1.call-done = f32[128,512]{1,0:T(8,128)} async-done(((f32[1024,512]{1,0:T(8,128)}), f32[128,512]{1,0:T(8,128)}) %reduce-scatter.8.cloned.1.call-update) | async-done | bytes 262160 | tf_op jit(solution)/shard_map/reduce_scatter | solution.py:35
  124.8 37.8 %reduce-scatter.6.cloned.1.call-done = f32[128,512]{1,0:T(8,128)} async-done(((f32[1024,512]{1,0:T(8,128)}), f32[128,512]{1,0:T(8,128)}) %reduce-scatter.6.cloned.1.call-update) | async-done | bytes 262160 | tf_op jit(solution)/shard_map/reduce_scatter | solution.py:34
  162.7 1.8 multiply_convert_fusion.2
  164.4 0.0 all-gather.8.cloned.1.call-update
  164.5 0.0 reduce-scatter.10.cloned.1.call-start
  164.5 28.6 %all-gather.8.cloned.1.call-done = bf16[1024,512]{1,0:T(8,128)(2,1)} async-done(((bf16[128,512]{1,0:T(8,128)(2,1)}), bf16[1024,512]{1,0:T(8,128)(2,1)}) %all-gather.8.cloned.1.call-update) | async-done | bytes 1048592 | tf_op jit(solution)/shard_map/all_gather | solution.py:38
  193.1 4.4 fusion.5
  197.5 0.0 reduce-scatter.10.cloned.1.call-update
  197.5 0.0 all-gather.10.cloned.1.call-start
  197.6 224.9 %reduce-scatter.10.cloned.1.call-done = f32[32,1024]{1,0:T(8,128)} async-done(((f32[1024,1024]{1,0:T(8,128)}), f32[32,1024]{1,0:T(8,128)}) %reduce-scatter.10.cloned.1.call-update) | async-done | bytes 131088 | tf_op jit(solution)/shard_map/reduce_scatter | solution.py:42
  422.5 1.7 subtract_convert_fusion
  424.1 0.0 all-gather.10.cloned.1.call-update
  424.2 0.0 reduce-scatter.12.cloned.1.call-start
  424.2 77.6 %all-gather.10.cloned.1.call-done = bf16[1024,1024]{1,0:T(8,128)(2,1)} async-done(((bf16[32,1024]{1,0:T(8,128)(2,1)}), bf16[1024,1024]{1,0:T(8,128)(2,1)}) %all-gather.10.cloned.1.call-update) | async-done | bytes 2097168 | tf_op jit(solution)/shard_map/all_gather | solution.py:46
  501.8 4.2 fusion.6
  506.0 0.0 reduce-scatter.12.cloned.1.call-update
  506.0 0.0 all-gather.12.cloned.1.call-start
  506.1 28.7 %reduce-scatter.12.cloned.1.call-done = f32[128,512]{1,0:T(8,128)} async-done(((f32[1024,512]{1,0:T(8,128)}), f32[128,512]{1,0:T(8,128)}) %reduce-scatter.12.cloned.1.call-update) | async-done | bytes 262160 | tf_op jit(solution)/shard_map/reduce_scatter | solution.py:49
  534.7 1.9 multiply_convert_fusion
  536.6 0.0 all-gather.12.cloned.1.call-update
  536.6 0.0 all-gather.14.cloned.1.call-start
  536.7 0.7 all-gather.14.cloned.1.call-update
  537.4 0.0 reduce-scatter.14.cloned.1.call-start
  537.4 27.9 %all-gather.12.cloned.1.call-done = bf16[1024,512]{1,0:T(8,128)(2,1)} async-done(((bf16[128,512]{1,0:T(8,128)(2,1)}), bf16[1024,512]{1,0:T(8,128)(2,1)}) %all-gather.12.cloned.1.call-update) | async-done | bytes 1048592 | tf_op jit(solution)/shard_map/all_gather | solution.py:52
  565.4 4.8 fusion.7
  570.1 23.4 %all-gather.14.cloned.1.call-done = bf16[1024,512]{1,0:T(8,128)(2,1)} async-done(((bf16[128,512]{1,0:T(8,128)(2,1)}), bf16[1024,512]{1,0:T(8,128)(2,1)}) %all-gather.14.cloned.1.call-update) | async-done | bytes 1048592 | tf_op jit(solution)/shard_map/all_gather | solution.py:53
  593.5 6.1 convolution_add_fusion
  599.6 0.0 reduce-scatter.14.cloned.1.call-update
  599.6 4.2 convolution_convert_fusion
  603.8 0.0 copy-done.2
  603.8 2.3 fusion.1
  606.1 2.3 copy.11
  608.4 3.5 fusion
  611.9 2.3 copy.10
  614.1 210.7 %reduce-scatter.14.cloned.1.call-done = f32[32,1024]{1,0:T(8,128)} async-done(((f32[1024,1024]{1,0:T(8,128)}), f32[32,1024]{1,0:T(8,128)}) %reduce-scatter.14.cloned.1.call-update) | async-done | bytes 131088 | tf_op jit(solution)/shard_map/reduce_scatter | solution.py:60
  824.8 1.5 convert_element_type.42
  (5 shorter events, 0.0 us)
Async XLA Ops:
  7.2 185.9 %copy-start = (bf16[512,1024]{1,0:T(8,128)(2,1)S(1)}, bf16[512,1024]{1,0:T(8,128)(2,1)}, u32[]{:S(2)}) copy-start(bf16[512,1024]{1,0:T(8,128)(2,1)} %param.9) | copy-start | bytes 3145732
  7.2 84.5 %all-gather.6.cloned.1.call-start = ((), (), s32[]{:S(2)}) async-start(), calls=%async_computation.5 | async-start | bytes 2162688 | tf_op jit(solution)/shard_map/all_gather | solution.py:30
  7.9 116.9 %reduce-scatter.8.cloned.1.call-start = ((), (), s32[]{:S(2)}) async-start(), calls=%async_computation.7 | async-start | bytes 2359296 | tf_op jit(solution)/shard_map/reduce_scatter | solution.py:35
  96.1 1.6 copy-start.1
  96.1 66.5 %reduce-scatter.6.cloned.1.call-start = ((), (), s32[]{:S(2)}) async-start(), calls=%async_computation.6 | async-start | bytes 2359296 | tf_op jit(solution)/shard_map/reduce_scatter | solution.py:34
  101.5 91.6 %all-gather.8.cloned.1.call-start = ((), (), s32[]{:S(2)}) async-start(), calls=%async_computation.8 | async-start | bytes 1179648 | tf_op jit(solution)/shard_map/all_gather | solution.py:38
  164.5 258.0 %reduce-scatter.10.cloned.1.call-start = ((), (), s32[]{:S(2)}) async-start(), calls=%async_computation.9 | async-start | bytes 4325376 | tf_op jit(solution)/shard_map/reduce_scatter | solution.py:42
  197.5 304.3 %all-gather.10.cloned.1.call-start = ((), (), s32[]{:S(2)}) async-start(), calls=%async_computation.10 | async-start | bytes 2162688 | tf_op jit(solution)/shard_map/all_gather | solution.py:46
  424.2 110.6 %reduce-scatter.12.cloned.1.call-start = ((), (), s32[]{:S(2)}) async-start(), calls=%async_computation.11 | async-start | bytes 2359296 | tf_op jit(solution)/shard_map/reduce_scatter | solution.py:49
  506.0 28.7 %copy-start.3 = (f32[128,512]{1,0:T(8,128)S(1)}, f32[128,512]{1,0:T(8,128)}, u32[]{:S(2)}) copy-start(f32[128,512]{1,0:T(8,128)} %reduce-scatter.8.cloned.1.call-done) | copy-start | bytes 786436
  506.0 59.3 %all-gather.12.cloned.1.call-start = ((), (), s32[]{:S(2)}) async-start(), calls=%async_computation.12 | async-start | bytes 1179648 | tf_op jit(solution)/shard_map/all_gather | solution.py:52
  536.6 56.9 %all-gather.14.cloned.1.call-start = ((), (), s32[]{:S(2)}) async-start(), calls=%async_computation.13 | async-start | bytes 1179648 | tf_op jit(solution)/shard_map/all_gather | solution.py:53
  537.4 287.5 %reduce-scatter.14.cloned.1.call-start = ((), (), s32[]{:S(2)}) async-start(), calls=%async_computation.14 | async-start | bytes 4325376 | tf_op jit(solution)/shard_map/reduce_scatter | solution.py:60
  599.6 4.2 copy-start.2
Sparse Core Ops, SparseCore 0:
  10.6 81.0 all-gather.5
  96.3 28.5 reduce-scatter.7
  127.4 35.2 reduce-scatter.5
  165.0 28.0 all-gather.7
  197.6 224.8 reduce-scatter.9
  425.5 76.2 all-gather.9
  506.1 28.5 reduce-scatter.11
  537.2 28.1 all-gather.11
  567.8 25.6 all-gather.13
  599.7 225.0 reduce-scatter.13
where the time goes:
time: 834 us; the launch traced here: 833 us
  waiting for transfers between devices  768 us (92%)
  matrix products  37.6 us (5%)
  between operations  14.2 us (2%)
    reduce_scatter x1, waiting for transfers between devices, body(): lax.psum_scatter(result_part, 'col', scatter_dimension=0, tiled=True)  225 us
    reduce_scatter x1, waiting for transfers between devices, body(): lax.psum_scatter(input_grad_part, 'col', scatter_dimension=0, tiled=True)  211 us
    all_gather x1, waiting for transfers between devices, body(): tokens_all = lax.all_gather(inputs, 'col', axis=0, tiled=True)  83.7 us
    all_gather x1, waiting for transfers between devices, body(): error_all = lax.all_gather(error_own, 'col', axis=0, tiled=True)  77.6 us
    reduce_scatter x1, waiting for transfers between devices, body(): lax.psum_scatter(gate_part, 'row', scatter_dimension=0, tiled=True)  37.8 us
    reduce_scatter x1, waiting for transfers between devices, body(): lax.psum_scatter(hidden_grad_part, 'row', scatter_dimension=0, tiled=True)  28.7 us
    all_gather x1, waiting for transfers between devices, body(): hidden_all = lax.all_gather(hidden_own, 'row', axis=0, tiled=True)  28.6 us
    all_gather x1, waiting for transfers between devices, body(): lax.all_gather(gate_grad_own, 'row', axis=0, tiled=True)  27.9 us
  transfers between devices with their start and end apart: 10, of which 10 were waited for; matrix products, arithmetic and copies ran while one was open for 3% of the time, Pallas kernels for 0%

commit v1 on v0

--- a/solution.py
+++ b/solution.py
@@ -2,6 +2,7 @@
 import jax.numpy as jnp
 from jax import lax
 from jax.sharding import PartitionSpec as P
+from jax.lax import all_to_all, axis_size
 
 
 def contract_first(left, right):
@@ -43,7 +44,9 @@
     target_own = lax.dynamic_slice_in_dim(target, offset, tok_col, 0)
     error_own = (result_own - target_own.astype(jnp.float32)).astype(jnp.bfloat16)
     output = result_own.astype(jnp.bfloat16)
-    error_all = lax.all_gather(error_own, "col", axis=0, tiled=True)
+    error_all = jnp.concatenate(
+        all_to_all(jnp.stack([error_own for _ in range(axis_size("col"))], 0), "col", 0, 0), 0
+    )
     grad_down_weight = contract_first(hidden_all, error_all).astype(jnp.bfloat16)
     hidden_grad_part = contract_last(error_all, down_weight)
     hidden_grad = lax.psum_scatter(hidden_grad_part, "row", scatter_dimension=0, tiled=True)

time: 834 us -> 808 us (0.969)
  waiting for transfers between devices: 768 us -> 691 us
  blocking collectives: 0 us -> 52 us
    all_gather x1 -> x0, waiting for transfers between devices: 77.6 us -> none  [body(): error_all = lax.all_gather(error_own, 'col', axis=0, tiled=True)]
    all_to_all x0 -> x1, blocking collectives: none -> 52 us  [body(): all_to_all(jnp.stack([error_own for _ in range(axis_size('col'))], 0), 'c...]
  transfers between devices with their start and end apart: 10 -> 9, of which waited for: 10 -> 9; matrix products, arithmetic and copies ran while one was open for 3% -> 3% of each run, Pallas kernels for 0% -> 0%
where the time goes in v1:
time: 808 us; the launch traced here: 807 us
  waiting for transfers between devices  691 us (86%)
  blocking collectives  52 us (6%)
  matrix products  36.1 us (4%)
  between operations  13.9 us (2%)
    reduce_scatter x1, waiting for transfers between devices, body(): lax.psum_scatter(result_part, 'col', scatter_dimension=0, tiled=True)  225 us
    reduce_scatter x1, waiting for transfers between devices, body(): lax.psum_scatter(input_grad_part, 'col', scatter_dimension=0, tiled=True)  211 us
    all_gather x1, waiting for transfers between devices, body(): tokens_all = lax.all_gather(inputs, 'col', axis=0, tiled=True)  83.7 us
    all_to_all x1, blocking collectives, body(): all_to_all(jnp.stack([error_own for _ in range(axis_size('col'))], 0), 'c...  52 us
    reduce_scatter x1, waiting for transfers between devices, body(): lax.psum_scatter(gate_part, 'row', scatter_dimension=0, tiled=True)  37.8 us
    reduce_scatter x1, waiting for transfers between devices, body(): lax.psum_scatter(hidden_grad_part, 'row', scatter_dimension=0, tiled=True)  28.6 us
    all_gather x1, waiting for transfers between devices, body(): hidden_all = lax.all_gather(hidden_own, 'row', axis=0, tiled=True)  28.6 us
    all_gather x1, waiting for transfers between devices, body(): lax.all_gather(gate_grad_own, 'row', axis=0, tiled=True)  27.9 us
  transfers between devices with their start and end apart: 9, of which 9 were waited for; matrix products, arithmetic and copies ran while one was open for 3% of the time, Pallas kernels for 0%

profile of v1, /device:TPU:4, one launch (start us, length us, event | category | flops | bytes accessed | tf_op | source)
XLA Modules:
  0.0 807.4 jit_solution(14259323960396147954)
XLA Ops:
  7.2 0.0 copy-start
  7.2 0.0 all-gather.5.cloned.1.call-start
  7.2 0.7 all-gather.5.cloned.1.call-update
  7.9 0.0 reduce-scatter.8.cloned.1.call-start
  8.0 83.7 %all-gather.5.cloned.1.call-done = bf16[1024,1024]{1,0:T(8,128)(2,1)} async-done(((bf16[32,1024]{1,0:T(8,128)(2,1)}), bf16[1024,1024]{1,0:T(8,128)(2,1)}) %all-gather.5.cloned.1.call-update) | async-done | bytes 2097168 | tf_op jit(solution)/shard_map/all_gather | solution.py:31
  91.7 4.4 fusion.4
  96.1 0.0 reduce-scatter.8.cloned.1.call-update
  96.1 0.0 reduce-scatter.6.cloned.1.call-start
  96.2 1.5 copy-done.1
  97.7 3.8 fusion.3
  101.5 0.0 reduce-scatter.6.cloned.1.call-update
  101.5 0.0 all-gather.7.cloned.1.call-start
  101.6 23.3 %reduce-scatter.8.cloned.1.call-done = f32[128,512]{1,0:T(8,128)} async-done(((f32[1024,512]{1,0:T(8,128)}), f32[128,512]{1,0:T(8,128)}) %reduce-scatter.8.cloned.1.call-update) | async-done | bytes 262160 | tf_op jit(solution)/shard_map/reduce_scatter | solution.py:36
  124.9 37.8 %reduce-scatter.6.cloned.1.call-done = f32[128,512]{1,0:T(8,128)} async-done(((f32[1024,512]{1,0:T(8,128)}), f32[128,512]{1,0:T(8,128)}) %reduce-scatter.6.cloned.1.call-update) | async-done | bytes 262160 | tf_op jit(solution)/shard_map/reduce_scatter | solution.py:35
  162.7 1.8 multiply_convert_fusion.2
  164.4 0.0 all-gather.7.cloned.1.call-update
  164.5 0.0 reduce-scatter.10.cloned.1.call-start
  164.5 28.6 %all-gather.7.cloned.1.call-done = bf16[1024,512]{1,0:T(8,128)(2,1)} async-done(((bf16[128,512]{1,0:T(8,128)(2,1)}), bf16[1024,512]{1,0:T(8,128)(2,1)}) %all-gather.7.cloned.1.call-update) | async-done | bytes 1048592 | tf_op jit(solution)/shard_map/all_gather | solution.py:39
  193.1 4.4 fusion.5
  197.5 0.0 reduce-scatter.10.cloned.1.call-update
  197.5 0.0 reduce-scatter.12.cloned.1.call-start
  197.6 225.1 %reduce-scatter.10.cloned.1.call-done = f32[32,1024]{1,0:T(8,128)} async-done(((f32[1024,1024]{1,0:T(8,128)}), f32[32,1024]{1,0:T(8,128)}) %reduce-scatter.10.cloned.1.call-update) | async-done | bytes 131088 | tf_op jit(solution)/shard_map/reduce_scatter | solution.py:43
  422.7 1.6 subtract_convert_fusion
  424.3 0.2 stack.2
  424.6 52.0 %all_to_all.5 = bf16[32,32,1024]{2,1,0:T(8,128)(2,1)S(1)} all-to-all(bf16[32,32,1024]{2,1,0:T(8,128)(2,1)S(1)} %stack.2), channel_id=1, replica_groups=mesh['row'=8,'col'=32] {'col'}, dimensions={0} | all-to-all | bytes 4194304 | tf_op jit(solution)/shard_map/all_to_all | solution.py:48
  476.5 1.4 copy-done.2
  477.9 2.6 fusion.6
  480.5 0.0 reduce-scatter.12.cloned.1.call-update
  480.5 0.0 all-gather.9.cloned.1.call-start
  480.6 28.6 %reduce-scatter.12.cloned.1.call-done = f32[128,512]{1,0:T(8,128)} async-done(((f32[1024,512]{1,0:T(8,128)}), f32[128,512]{1,0:T(8,128)}) %reduce-scatter.12.cloned.1.call-update) | async-done | bytes 262160 | tf_op jit(solution)/shard_map/reduce_scatter | solution.py:52
  509.2 0.0 copy-done.4
  509.2 1.9 multiply_convert_fusion
  511.0 0.0 all-gather.9.cloned.1.call-update
  511.0 0.0 all-gather.11.cloned.1.call-start
  511.1 0.7 all-gather.11.cloned.1.call-update
  511.8 0.0 reduce-scatter.14.cloned.1.call-start
  511.8 27.9 %all-gather.9.cloned.1.call-done = bf16[1024,512]{1,0:T(8,128)(2,1)} async-done(((bf16[128,512]{1,0:T(8,128)(2,1)}), bf16[1024,512]{1,0:T(8,128)(2,1)}) %all-gather.9.cloned.1.call-update) | async-done | bytes 1048592 | tf_op jit(solution)/shard_map/all_gather | solution.py:55
  539.8 4.8 fusion.7
  544.6 23.4 %all-gather.11.cloned.1.call-done = bf16[1024,512]{1,0:T(8,128)(2,1)} async-done(((bf16[128,512]{1,0:T(8,128)(2,1)}), bf16[1024,512]{1,0:T(8,128)(2,1)}) %all-gather.11.cloned.1.call-update) | async-done | bytes 1048592 | tf_op jit(solution)/shard_map/all_gather | solution.py:56
  567.9 6.1 convolution_add_fusion
  574.0 0.0 reduce-scatter.14.cloned.1.call-update
  574.0 4.2 convolution_convert_fusion
  578.3 2.3 fusion.1
  580.5 2.3 copy.11
  582.8 3.5 fusion
  586.3 2.3 copy.10
  588.6 210.8 %reduce-scatter.14.cloned.1.call-done = f32[32,1024]{1,0:T(8,128)} async-done(((f32[1024,1024]{1,0:T(8,128)}), f32[32,1024]{1,0:T(8,128)}) %reduce-scatter.14.cloned.1.call-update) | async-done | bytes 131088 | tf_op jit(solution)/shard_map/reduce_scatter | solution.py:63
  799.3 1.5 convert_element_type.42
  (6 shorter events, 0.0 us)
Async XLA Ops:
  7.2 185.9 %copy-start = (bf16[512,1024]{1,0:T(8,128)(2,1)S(1)}, bf16[512,1024]{1,0:T(8,128)(2,1)}, u32[]{:S(2)}) copy-start(bf16[512,1024]{1,0:T(8,128)(2,1)} %param.9) | copy-start | bytes 3145732
  7.2 84.5 %all-gather.5.cloned.1.call-start = ((), (), s32[]{:S(2)}) async-start(), calls=%async_computation.6 | async-start | bytes 2162688 | tf_op jit(solution)/shard_map/all_gather | solution.py:31
  7.9 116.9 %reduce-scatter.8.cloned.1.call-start = ((), (), s32[]{:S(2)}) async-start(), calls=%async_computation.8 | async-start | bytes 2359296 | tf_op jit(solution)/shard_map/reduce_scatter | solution.py:36
  96.1 1.6 copy-start.1
  96.1 66.5 %reduce-scatter.6.cloned.1.call-start = ((), (), s32[]{:S(2)}) async-start(), calls=%async_computation.7 | async-start | bytes 2359296 | tf_op jit(solution)/shard_map/reduce_scatter | solution.py:35
  101.5 91.6 %all-gather.7.cloned.1.call-start = ((), (), s32[]{:S(2)}) async-start(), calls=%async_computation.9 | async-start | bytes 1179648 | tf_op jit(solution)/shard_map/all_gather | solution.py:39
  164.5 258.2 %reduce-scatter.10.cloned.1.call-start = ((), (), s32[]{:S(2)}) async-start(), calls=%async_computation.10 | async-start | bytes 4325376 | tf_op jit(solution)/shard_map/reduce_scatter | solution.py:43
  197.5 311.6 %reduce-scatter.12.cloned.1.call-start = ((), (), s32[]{:S(2)}) async-start(), calls=%async_computation.11 | async-start | bytes 2359296 | tf_op jit(solution)/shard_map/reduce_scatter | solution.py:52
  476.5 1.4 copy-start.2
  480.5 28.7 %copy-start.4 = (f32[128,512]{1,0:T(8,128)S(1)}, f32[128,512]{1,0:T(8,128)}, u32[]{:S(2)}) copy-start(f32[128,512]{1,0:T(8,128)} %reduce-scatter.8.cloned.1.call-done) | copy-start | bytes 786436
  480.5 59.3 %all-gather.9.cloned.1.call-start = ((), (), s32[]{:S(2)}) async-start(), calls=%async_computation.12 | async-start | bytes 1179648 | tf_op jit(solution)/shard_map/all_gather | solution.py:55
  511.0 56.9 %all-gather.11.cloned.1.call-start = ((), (), s32[]{:S(2)}) async-start(), calls=%async_computation.13 | async-start | bytes 1179648 | tf_op jit(solution)/shard_map/all_gather | solution.py:56
  511.8 287.5 %reduce-scatter.14.cloned.1.call-start = ((), (), s32[]{:S(2)}) async-start(), calls=%async_computation.14 | async-start | bytes 4325376 | tf_op jit(solution)/shard_map/reduce_scatter | solution.py:63
  574.0 4.2 copy-start.3
Sparse Core Ops, SparseCore 0:
  10.6 81.0 all-gather.4
  96.3 28.5 reduce-scatter.7
  127.4 35.2 reduce-scatter.5
  165.0 28.0 all-gather.6
  197.7 224.9 reduce-scatter.9
  480.7 28.4 reduce-scatter.11
  511.6 28.1 all-gather.8
  542.2 25.6 all-gather.10
  574.2 225.1 reduce-scatter.13
